TPU v7x, 256 devices: a whole 4x4x8 slice. The times are simulated.
256 devices in a mesh: wide: 32 (over z, y), slab: 8 (over x, core).
Axes of the slice: x: 4, y: 4, z: 8, core: 2. Of those that a mesh axis runs over, the one named last changes fastest.
Arguments:
- thermal_state: float32 [32, 128, 32, 1024], P('wide', 'slab'), may hold values from -5 to 5
- thermal_spreading_rate: bfloat16 [32, 128, 32, 1024], P('wide', 'slab'), may hold values from 0.5 to 1.5
- flow_speed_vector: bfloat16 [3, 32, 128, 32, 1024], P(None, 'wide', 'slab'), may hold values from -0.796875 to 0.796875
- interface_guess: float32 [32, 2048], P('wide', 'slab'), may hold values from -4 to 4
- partner_facing_rows: int32 [32, 2048], P('wide', 'slab'), may hold values from 0 to 2047, each once within a row
- mismatch_change_matrix: float32 [32, 2048, 128], P('wide', 'slab'), may hold values from -5 to 5
- output_change_matrix: float32 [32, 2048, 128], P('wide', 'slab'), may hold values from -1.8 to 1.8
Outputs:
- temperature_out: float32 [32, 128, 32, 1024], P('wide', 'slab')
- updated_interface_guess: float32 [32, 2048], P('wide', 'slab')
- unitary_basis_factor: float32 [32, 2048, 128], P('wide', 'slab')
Inputs may be any that keep to these rules, and one draw needn't show every extreme that they name: `partner_facing_rows`: each partition's rows of matching are a permutation of its partner's interface rows.
All inputs are finite; a program needn't handle non-finite values.
Results may differ from a plain program's by a relative error of at most 0.0003.
Values may be sent and summed in bfloat16 or wider, within the bound.
No kernel may reach another device: no remote copies, remote signals or barrier semaphores. Data moves between devices by JAX's collectives and lax.ppermute only.
A program may use at most 64 MiB of HBM per device.

v0:
```python
import math
import jax
import jax.numpy as jnp
from jax import lax
from jax.sharding import PartitionSpec as P

INTERFACE_STRIP = 64
SWEEPS = 4
STEP_SIZE = 0.11


def padded(cells, sides, width):
    for axis, dim in sides:
        count = lax.axis_size(axis)
        ends = count - 1
        head = lax.slice_in_dim(cells, 0, width, axis=dim)
        tail = lax.slice_in_dim(cells, cells.shape[dim] - width, cells.shape[dim], axis=dim)
        cells = jnp.concatenate(
            [
                lax.ppermute(tail, axis, [(i, (i + 1) % count) for i in range(ends)]),
                cells,
                lax.ppermute(head, axis, [((i + 1) % count, i) for i in range(ends)]),
            ],
            axis=dim,
        )
    return cells


def partner(value, axis, stride):
    mask = 2**stride
    pairs = [(source, source ^ mask) for source in range(lax.axis_size(axis))]
    return lax.ppermute(value, axis, pairs)


def gather_sum(value, axes):
    count = lax.axis_size(axes)
    copies = jnp.broadcast_to(value[None], (count, *value.shape))
    return jnp.sum(lax.all_to_all(copies, axes, 0, 0, tiled=True), axis=0)


def sum_everywhere(square):
    rows = square.shape[0] // lax.axis_size("slab")
    blocks = square.reshape(-1, rows, square.shape[1])
    mine = jnp.sum(lax.all_to_all(blocks, "slab", 0, 0, tiled=True), axis=0)
    mine = gather_sum(mine, "wide")
    copies = jnp.broadcast_to(mine[None], blocks.shape)
    return lax.all_to_all(copies, "slab", 0, 0, tiled=True).reshape(square.shape)


def surround_wrapper(block_rows, mirror_layer):
    bottom = jnp.zeros((block_rows.shape[0], 1, block_rows.shape[2]), block_rows.dtype)
    stacked = jnp.concatenate([bottom, block_rows, mirror_layer[:, None, :]], axis=1)
    return jnp.pad(stacked, ((0, 0), (0, 0), (1, 1)))


def march_forward(bordered_array, diffuse_subdomain, subdomain_flow_speed):
    centre = bordered_array[1:-1, 1:-1, 1:-1]
    plus_first = bordered_array[2:, 1:-1, 1:-1]
    minus_first = bordered_array[:-2, 1:-1, 1:-1]
    plus_second = bordered_array[1:-1, 2:, 1:-1]
    minus_second = bordered_array[1:-1, :-2, 1:-1]
    plus_third = bordered_array[1:-1, 1:-1, 2:]
    minus_third = bordered_array[1:-1, 1:-1, :-2]
    spread = (
        plus_first
        + minus_first
        + plus_second
        + minus_second
        + plus_third
        + minus_third
        - 6.0 * centre
    )
    carried = 0.5 * (
        subdomain_flow_speed[0].astype(jnp.float32) * (plus_first - minus_first)
        + subdomain_flow_speed[1].astype(jnp.float32) * (plus_second - minus_second)
        + subdomain_flow_speed[2].astype(jnp.float32) * (plus_third - minus_third)
    )
    return centre + STEP_SIZE * (diffuse_subdomain.astype(jnp.float32) * spread - carried)


def shards(
    thermal_state,
    thermal_spreading_rate,
    flow_speed_vector,
    interface_guess,
    partner_facing_rows,
    mismatch_change_matrix,
    output_change_matrix,
):
    subdomain_thermal_state = thermal_state[0]
    diffuse_subdomain = thermal_spreading_rate[0]
    subdomain_flow_speed = flow_speed_vector[:, 0]
    layer_stack = subdomain_thermal_state.shape[0]
    vertical_extent = subdomain_thermal_state.shape[1]
    rows_dev = interface_guess.shape[1]
    mirror_layer = jnp.repeat(interface_guess[0].reshape(layer_stack, -1), INTERFACE_STRIP, axis=1)
    panel = mismatch_change_matrix[0]
    gram_local = lax.dot_general(
        panel,
        panel,
        (((0,), (0,)), ((), ())),
        precision=lax.Precision.HIGHEST,
        preferred_element_type=jnp.float32,
    )
    ghost_padded = jnp.pad(mirror_layer, ((1, 1), (0, 0)))
    for sweep in range(SWEEPS):
        widened_array = padded(subdomain_thermal_state, (("slab", 0),), 1)
        subdomain_thermal_state = march_forward(
            surround_wrapper(widened_array, ghost_padded), diffuse_subdomain, subdomain_flow_speed
        )
    face_means = jnp.mean(
        subdomain_thermal_state[:, vertical_extent - 1, :].reshape(
            layer_stack, -1, INTERFACE_STRIP
        ),
        axis=2,
    )
    face_means = face_means.reshape(1, rows_dev)
    top_bit = lax.axis_size("wide").bit_length() - 2
    partner_own = partner(face_means, "wide", top_bit)
    partner_all = lax.all_gather(partner_own, "slab", axis=1, tiled=True)
    tilde = jnp.take(partner_all[0], partner_facing_rows[0], axis=0)
    resid = tilde - interface_guess[0]
    proj_local = jnp.dot(
        resid, panel, precision=lax.Precision.HIGHEST, preferred_element_type=jnp.float32
    )
    gram_matrix = sum_everywhere(gram_local)
    projection = gather_sum(proj_local, ("wide", "slab"))
    lower_factor = jnp.linalg.cholesky(gram_matrix)
    half_solve = lax.linalg.triangular_solve(
        lower_factor, projection[:, None], left_side=True, lower=True
    )
    coefficients = -lax.linalg.triangular_solve(
        lower_factor, half_solve, left_side=True, lower=True, transpose_a=True
    )[:, 0]
    update = jnp.dot(
        output_change_matrix[0],
        coefficients,
        precision=lax.Precision.HIGHEST,
        preferred_element_type=jnp.float32,
    )
    updated_interface_guess = tilde + update
    total_rows = rows_dev * lax.axis_size("slab") * lax.axis_size("wide")
    scaled = lax.linalg.triangular_solve(
        lower_factor, panel, left_side=False, lower=True, transpose_a=True
    )
    unitary_basis_factor = math.sqrt(total_rows) * scaled
    return (
        subdomain_thermal_state[None],
        updated_interface_guess[None],
        unitary_basis_factor[None],
    )


def solution(mesh):
    return jax.shard_map(
        shards,
        mesh=mesh,
        in_specs=(
            P("wide", "slab", None, None),
            P("wide", "slab", None, None),
            P(None, "wide", "slab", None, None),
            P("wide", "slab"),
            P("wide", "slab"),
            P("wide", "slab", None),
            P("wide", "slab", None),
        ),
        out_specs=(P("wide", "slab", None, None), P("wide", "slab"), P("wide", "slab", None)),
        check_vma=False,
    )
```

profile of v0, /device:TPU:1, one launch (start us, length us, event | category | flops | bytes accessed | tf_op | source)
XLA Modules:
  0.0 155.6 jit_solution(3249432732262084621)
XLA Ops:
  0.6 1.0 slice_bitcast_fusion
  1.7 5.1 %collective-permute-start = (f32[1,32,1024]{2,1,0:T(8,128)S(1)}, f32[1,32,1024]{2,1,0:T(8,128)S(1)}, u32[]{:S(2)}, u32[]{:S(2)}) collective-permute-start(f32[1,32,1024]{2,1,0:T(8,128)S(1)} %get-tuple-element.22), channel_id=1, source_target_pairs={{1,0},{2,1},{3,2},{4,3},{5,4},{6,5},{7,6},{9,8},{10,9},{11,10},{12... | collective-permute-start | bytes 393224 | tf_op jit(solution)/shard_map/ppermute | solution.py:22
  6.8 1.9 %collective-permute-start.1 = (f32[1,32,1024]{2,1,0:T(8,128)S(1)}, f32[1,32,1024]{2,1,0:T(8,128)S(1)}, u32[]{:S(2)}, u32[]{:S(2)}) collective-permute-start(f32[1,32,1024]{2,1,0:T(8,128)S(1)} %get-tuple-element.21), channel_id=1, source_target_pairs={{0,1},{1,2},{2,3},{3,4},{4,5},{5,6},{6,7},{8,9},{9,10},{10,11},{11... | collective-permute-start | bytes 393224 | tf_op jit(solution)/shard_map/ppermute | solution.py:20
  9.3 1.3 reduce.12
  11.0 0.7 copy-done.15
  11.7 2.3 %pad_maximum_fusion.3 = f32[18,34,1024]{2,1,0:T(8,128)S(1)} fusion(f32[18,1,1024]{2,1,0:T(1,128)S(1)} %broadcast_in_dim.48, f32[1,32,1024]{2,1,0:T(8,128)S(1)} %collective-permute-done, f32[16,32,1024]{2,1,0:T(8,128)} %bitcast.102, f32[1,32,1024]{2,1,0:T(8,128)} %copy-done.15, f32[34]{0:T(128)S(1)} %pad.74.clone), kind=kLoop, calls=%fused_computation.4 | loop fusion | flops 2506752 | bytes 4939912 | tf_op jit(solution)/shard_map/concatenate | solution.py:52
  14.6 7.1 %fusion.2 = f32[16,32,1024]{2,1,0:T(8,128)S(1)} fusion(f32[16,32,1024]{2,1,0:T(8,128)} %bitcast.103, f32[18,34,1024]{2,1,0:T(8,128)S(1)} %pad_maximum_fusion.3, f32[1,32,1024]{2,1,0:T(8,128)} %copy-done.14, f32[1,32,1024]{2,1,0:T(8,128)S(1)} %copy-done.16, f32[18,1,1024]{2,1,0:T(1,128)S(1)} %broadcast_in_dim.48, bf16[1,16,32,1024]{3,2,1,0:T(8,128)(2,1)S(1)} %copy-done.8, ...), kind=kLoop, calls=%fused_computation.35 | loop fusion | flops 18874368 | bytes 11231232 | tf_op jit(solution)/shard_map/add | solution.py:78
  21.7 1.3 copy-done.6
  23.0 0.7 fusion.61
  23.7 2.4 %collective-permute-start.2 = (f32[1,32,1024]{2,1,0:T(8,128)}, f32[1,32,1024]{2,1,0:T(8,128)}, u32[]{:S(2)}, u32[]{:S(2)}) collective-permute-start(f32[1,32,1024]{2,1,0:T(8,128)} %get-tuple-element.20), channel_id=1, source_target_pairs={{1,0},{2,1},{3,2},{4,3},{5,4},{6,5},{7,6},{9,8},{10,9},{11,10},{12... | collective-permute-start | bytes 393224 | tf_op jit(solution)/shard_map/ppermute | solution.py:22
  26.1 3.5 %collective-permute-start.3 = (f32[1,32,1024]{2,1,0:T(8,128)}, f32[1,32,1024]{2,1,0:T(8,128)}, u32[]{:S(2)}, u32[]{:S(2)}) collective-permute-start(f32[1,32,1024]{2,1,0:T(8,128)} %get-tuple-element.19), channel_id=1, source_target_pairs={{0,1},{1,2},{2,3},{3,4},{4,5},{5,6},{6,7},{8,9},{9,10},{10,11},{11... | collective-permute-start | bytes 393224 | tf_op jit(solution)/shard_map/ppermute | solution.py:20
  29.7 0.7 copy.21
  30.7 1.2 collective-permute-done.3
  31.9 2.2 %pad_maximum_fusion.2 = f32[18,34,1024]{2,1,0:T(8,128)S(1)} fusion(f32[18,1,1024]{2,1,0:T(1,128)S(1)} %broadcast_in_dim.48, f32[1,32,1024]{2,1,0:T(8,128)} %collective-permute-done.2, f32[16,32,1024]{2,1,0:T(8,128)} %copy-done.6, f32[1,32,1024]{2,1,0:T(8,128)} %collective-permute-done.3, f32[34]{0:T(128)S(1)} %pad.74.clone), kind=kLoop, calls=%fused_computation.3 | loop fusion | flops 2506752 | bytes 4939912 | tf_op jit(solution)/shard_map/concatenate | solution.py:52
  34.1 4.7 %fusion.5 = f32[16,32,1024]{2,1,0:T(8,128)S(1)} fusion(f32[16,32,1024]{2,1,0:T(8,128)S(1)} %copy-done.7, f32[18,34,1024]{2,1,0:T(8,128)S(1)} %pad_maximum_fusion.2, f32[1,32,1024]{2,1,0:T(8,128)} %collective-permute-done.2, f32[1,32,1024]{2,1,0:T(8,128)} %collective-permute-done.3, f32[18,1,1024]{2,1,0:T(1,128)S(1)} %broadcast_in_dim.48, ...), kind=kLoop, calls=%fused_computation.38 | loop fusion | flops 18874368 | bytes 11231232 | tf_op jit(solution)/shard_map/add | solution.py:78
  38.9 1.3 copy-done.4
  40.2 0.7 fusion.60
  40.9 1.9 %collective-permute-start.4 = (f32[1,32,1024]{2,1,0:T(8,128)}, f32[1,32,1024]{2,1,0:T(8,128)}, u32[]{:S(2)}, u32[]{:S(2)}) collective-permute-start(f32[1,32,1024]{2,1,0:T(8,128)} %get-tuple-element.18), channel_id=1, source_target_pairs={{1,0},{2,1},{3,2},{4,3},{5,4},{6,5},{7,6},{9,8},{10,9},{11,10},{12... | collective-permute-start | bytes 393224 | tf_op jit(solution)/shard_map/ppermute | solution.py:22
  42.8 4.4 %collective-permute-start.5 = (f32[1,32,1024]{2,1,0:T(8,128)}, f32[1,32,1024]{2,1,0:T(8,128)}, u32[]{:S(2)}, u32[]{:S(2)}) collective-permute-start(f32[1,32,1024]{2,1,0:T(8,128)} %get-tuple-element.17), channel_id=1, source_target_pairs={{0,1},{1,2},{2,3},{3,4},{4,5},{5,6},{6,7},{8,9},{9,10},{10,11},{11... | collective-permute-start | bytes 393224 | tf_op jit(solution)/shard_map/ppermute | solution.py:20
  47.2 0.9 fusion.37
  48.1 3.7 %all-to-all-start = ((f32[8,16,128]{2,1,0:T(8,128)}), f32[8,16,128]{2,1,0:T(8,128)S(1)}, u32[]{:S(2)}, u32[]{:S(2)}) async-start(f32[8,16,128]{2,1,0:T(8,128)} %fusion.37), calls=%async_computation | async-start | bytes 131072 | tf_op jit(solution)/shard_map/all_to_all | solution.py:44
  51.8 2.3 %pad_maximum_fusion.1 = f32[18,34,1024]{2,1,0:T(8,128)S(1)} fusion(f32[18,1,1024]{2,1,0:T(1,128)S(1)} %broadcast_in_dim.48, f32[1,32,1024]{2,1,0:T(8,128)} %collective-permute-done.4, f32[16,32,1024]{2,1,0:T(8,128)} %copy-done.4, f32[1,32,1024]{2,1,0:T(8,128)} %collective-permute-done.5, f32[34]{0:T(128)S(1)} %pad.74.clone), kind=kLoop, calls=%fused_computation.2 | loop fusion | flops 2506752 | bytes 4939912 | tf_op jit(solution)/shard_map/concatenate | solution.py:52
  54.4 4.7 %fusion.8 = f32[16,32,1024]{2,1,0:T(8,128)S(1)} fusion(f32[16,32,1024]{2,1,0:T(8,128)S(1)} %copy-done.5, f32[18,34,1024]{2,1,0:T(8,128)S(1)} %pad_maximum_fusion.1, f32[1,32,1024]{2,1,0:T(8,128)} %collective-permute-done.4, f32[1,32,1024]{2,1,0:T(8,128)} %collective-permute-done.5, f32[18,1,1024]{2,1,0:T(1,128)S(1)} %broadcast_in_dim.48, ...), kind=kLoop, calls=%fused_computation.41 | loop fusion | flops 18874368 | bytes 11231232 | tf_op jit(solution)/shard_map/add | solution.py:78
  59.1 1.3 copy-done.2
  60.4 0.7 fusion.59
  61.1 1.9 %collective-permute-start.6 = (f32[1,32,1024]{2,1,0:T(8,128)}, f32[1,32,1024]{2,1,0:T(8,128)}, u32[]{:S(2)}, u32[]{:S(2)}) collective-permute-start(f32[1,32,1024]{2,1,0:T(8,128)} %get-tuple-element.16), channel_id=1, source_target_pairs={{1,0},{2,1},{3,2},{4,3},{5,4},{6,5},{7,6},{9,8},{10,9},{11,10},{12... | collective-permute-start | bytes 393224 | tf_op jit(solution)/shard_map/ppermute | solution.py:22
  63.0 3.6 %collective-permute-start.7 = (f32[1,32,1024]{2,1,0:T(8,128)}, f32[1,32,1024]{2,1,0:T(8,128)}, u32[]{:S(2)}, u32[]{:S(2)}) collective-permute-start(f32[1,32,1024]{2,1,0:T(8,128)} %get-tuple-element.15), channel_id=1, source_target_pairs={{0,1},{1,2},{2,3},{3,4},{4,5},{5,6},{6,7},{8,9},{9,10},{10,11},{11... | collective-permute-start | bytes 393224 | tf_op jit(solution)/shard_map/ppermute | solution.py:20
  67.3 0.7 broadcast_in_dim.51
  68.0 11.3 %all-to-all-start.1 = ((f32[32,16,128]{2,1,0:T(8,128)}), f32[32,16,128]{2,1,0:T(8,128)}, u32[]{:S(2)}, u32[]{:S(2)}) async-start(f32[32,16,128]{2,1,0:T(8,128)} %broadcast_in_dim.51), calls=%async_computation.1 | async-start | bytes 524288 | tf_op jit(solution)/shard_map/all_to_all | solution.py:38
  79.4 2.3 %pad_maximum_fusion = f32[18,34,1024]{2,1,0:T(8,128)S(1)} fusion(f32[18,1,1024]{2,1,0:T(1,128)S(1)} %broadcast_in_dim.48, f32[1,32,1024]{2,1,0:T(8,128)} %collective-permute-done.6, f32[16,32,1024]{2,1,0:T(8,128)} %copy-done.2, f32[1,32,1024]{2,1,0:T(8,128)} %collective-permute-done.7, f32[34]{0:T(128)} %copy-done.20), kind=kLoop, calls=%fused_computation.1 | loop fusion | flops 2506752 | bytes 4939912 | tf_op jit(solution)/shard_map/concatenate | solution.py:52
  81.9 4.7 %fusion.11 = f32[16,32,1024]{2,1,0:T(8,128)S(1)} fusion(f32[16,32,1024]{2,1,0:T(8,128)S(1)} %copy-done.3, f32[18,34,1024]{2,1,0:T(8,128)S(1)} %pad_maximum_fusion, f32[1,32,1024]{2,1,0:T(8,128)} %collective-permute-done.6, f32[1,32,1024]{2,1,0:T(8,128)} %collective-permute-done.7, f32[18,1,1024]{2,1,0:T(1,128)S(1)} %broadcast_in_dim.48, ...), kind=kLoop, calls=%fused_computation.44 | loop fusion | flops 18874368 | bytes 11231232 | tf_op jit(solution)/shard_map/add | solution.py:78
  86.7 1.3 copy-done.12
  88.5 5.3 %collective-permute-start.8 = (f32[1,256]{1,0:T(1,128)S(1)}, f32[1,256]{1,0:T(1,128)S(1)}, u32[]{:S(2)}, u32[]{:S(2)}) collective-permute-start(f32[1,256]{1,0:T(1,128)S(1)} %div.18), channel_id=1, source_target_pairs={{0,128},{8,136},{16,144},{24,152},{32,160},{40,168},{48,176},{56,1... | collective-permute-start | bytes 3080 | tf_op jit(solution)/shard_map/ppermute | solution.py:32
  93.7 1.2 collective-permute-done.8
  95.0 11.7 %all_gather.3 = f32[1,2048]{1,0:T(1,128)S(1)} all-gather(f32[1,256]{1,0:T(1,128)S(1)} %collective-permute-done.8), channel_id=1, replica_groups=mesh['wide'=32,'slab'=8] {'slab'}, dimensions={1}, use_global_device_ids=true | all-gather | bytes 9216 | tf_op jit(solution)/shard_map/all_gather | solution.py:120
  106.6 1.7 %gather_fusion = f32[256]{0:T(256)S(1)} fusion(f32[2048]{0:T(1024)S(1)} %bitcast.101, s32[1024]{0:T(1024)S(1)} %pad_clamp_fusion), kind=kCustom, calls=%fused_computation | custom fusion | bytes 3072 | tf_op jit(solution)/shard_map/jit(_take)/gather | solution.py:121
  108.4 1.0 reduce_sum.38
  109.4 0.6 broadcast_in_dim.52
  110.0 3.4 %all-to-all-start.2 = ((f32[8,16,128]{2,1,0:T(8,128)}), f32[8,16,128]{2,1,0:T(8,128)S(1)}, u32[]{:S(2)}, u32[]{:S(2)}) async-start(f32[8,16,128]{2,1,0:T(8,128)} %broadcast_in_dim.52), calls=%async_computation.2 | async-start | bytes 131072 | tf_op jit(solution)/shard_map/all_to_all | solution.py:47
  113.6 4.7 %all-to-all-done.2 = f32[8,16,128]{2,1,0:T(8,128)S(1)} async-done(((f32[8,16,128]{2,1,0:T(8,128)}), f32[8,16,128]{2,1,0:T(8,128)S(1)}, u32[]{:S(2)}, u32[]{:S(2)}) %all-to-all-start.2) | async-done | bytes 65568 | tf_op jit(solution)/shard_map/all_to_all | solution.py:47
  118.3 0.7 broadcast_in_dim.54
  119.0 11.3 %all-to-all-start.3 = ((f32[256,1,128]{2,1,0:T(1,128)}), f32[256,1,128]{2,1,0:T(1,128)S(1)}, u32[]{:S(2)}, u32[]{:S(2)}) async-start(f32[256,1,128]{2,1,0:T(1,128)} %broadcast_in_dim.54), calls=%async_computation.3 | async-start | bytes 262144 | tf_op jit(solution)/shard_map/all_to_all | solution.py:38
  130.5 11.7 %cholesky.16 = f32[128,128]{1,0:T(8,128)S(1)} custom-call(f32[128,128]{1,0:T(8,128)S(1)} %fusion.45), custom_call_target="Cholesky" | custom-call | tf_op jit(solution)/shard_map/jit(cholesky)/cholesky | solution.py:128
  142.2 0.6 compare_reduce_fusion
  142.8 0.7 fusion.41
  143.5 9.8 %custom-call.10 = f32[1,128,128]{1,2,0:T(8,128)S(1)} custom-call(f32[1,128,128]{2,1,0:T(8,128)S(1)} %fusion.41), custom_call_target="InvertDiagBlocksLowerTriangular" | custom-call | tf_op jit(solution)/shard_map/triangular_solve | solution.py:132
  153.6 0.8 copy.25
  155.0 0.6 fusion.46
  (75 shorter events, 4.5 us)
Async XLA Ops:
  0.6 154.2 %copy-start = (f32[1,256,128]{2,1,0:T(8,128)S(1)}, f32[1,256,128]{2,1,0:T(8,128)}, u32[]{:S(2)}) copy-start(f32[1,256,128]{2,1,0:T(8,128)} %param.13) | copy-start | bytes 393220
  1.7 9.3 %collective-permute-start = (f32[1,32,1024]{2,1,0:T(8,128)S(1)}, f32[1,32,1024]{2,1,0:T(8,128)S(1)}, u32[]{:S(2)}, u32[]{:S(2)}) collective-permute-start(f32[1,32,1024]{2,1,0:T(8,128)S(1)} %get-tuple-element.22), channel_id=1, source_target_pairs={{1,0},{2,1},{3,2},{4,3},{5,4},{6,5},{7,6},{9,8},{10,9},{11,10},{12... | collective-permute-start | bytes 393224 | tf_op jit(solution)/shard_map/ppermute | solution.py:22
  6.8 4.2 %collective-permute-start.1 = (f32[1,32,1024]{2,1,0:T(8,128)S(1)}, f32[1,32,1024]{2,1,0:T(8,128)S(1)}, u32[]{:S(2)}, u32[]{:S(2)}) collective-permute-start(f32[1,32,1024]{2,1,0:T(8,128)S(1)} %get-tuple-element.21), channel_id=1, source_target_pairs={{0,1},{1,2},{2,3},{3,4},{4,5},{5,6},{6,7},{8,9},{9,10},{10,11},{11... | collective-permute-start | bytes 393224 | tf_op jit(solution)/shard_map/ppermute | solution.py:20
  11.0 40.8 %copy-start.20 = (f32[34]{0:T(128)}, f32[34]{0:T(128)S(1)}, u32[]{:S(2)}) copy-start(f32[34]{0:T(128)S(1)} %pad.74.clone) | copy-start | bytes 412
  11.0 0.7 copy-start.14
  11.0 0.7 copy-start.15
  11.7 2.6 %copy-start.1 = (bf16[3,1,16,32,1024]{4,3,2,1,0:T(8,128)(2,1)S(1)}, bf16[3,1,16,32,1024]{4,3,2,1,0:T(8,128)(2,1)}, u32[]{:S(2)}) copy-start(bf16[3,1,16,32,1024]{4,3,2,1,0:T(8,128)(2,1)} %param.9) | copy-start | bytes 9437188
  11.7 2.8 %copy-start.8 = (bf16[1,16,32,1024]{3,2,1,0:T(8,128)(2,1)S(1)}, bf16[1,16,32,1024]{3,2,1,0:T(8,128)(2,1)}, u32[]{:S(2)}) copy-start(bf16[1,16,32,1024]{3,2,1,0:T(8,128)(2,1)} %param.8) | copy-start | bytes 3145732
  11.7 2.8 %copy-start.16 = (f32[1,32,1024]{2,1,0:T(8,128)S(1)}, f32[1,32,1024]{2,1,0:T(8,128)}, u32[]{:S(2)}) copy-start(f32[1,32,1024]{2,1,0:T(8,128)} %copy-done.15) | copy-start | bytes 393220
  14.6 15.1 %copy-start.13 = (f32[1,256,128]{2,1,0:T(8,128)S(1)}, f32[1,256,128]{2,1,0:T(8,128)}, u32[]{:S(2)}) copy-start(f32[1,256,128]{2,1,0:T(8,128)} %param.12) | copy-start | bytes 393220
  21.7 1.3 copy-start.6
  23.7 6.9 %collective-permute-start.2 = (f32[1,32,1024]{2,1,0:T(8,128)}, f32[1,32,1024]{2,1,0:T(8,128)}, u32[]{:S(2)}, u32[]{:S(2)}) collective-permute-start(f32[1,32,1024]{2,1,0:T(8,128)} %get-tuple-element.20), channel_id=1, source_target_pairs={{1,0},{2,1},{3,2},{4,3},{5,4},{6,5},{7,6},{9,8},{10,9},{11,10},{12... | collective-permute-start | bytes 393224 | tf_op jit(solution)/shard_map/ppermute | solution.py:22
  26.1 5.7 %collective-permute-start.3 = (f32[1,32,1024]{2,1,0:T(8,128)}, f32[1,32,1024]{2,1,0:T(8,128)}, u32[]{:S(2)}, u32[]{:S(2)}) collective-permute-start(f32[1,32,1024]{2,1,0:T(8,128)} %get-tuple-element.19), channel_id=1, source_target_pairs={{0,1},{1,2},{2,3},{3,4},{4,5},{5,6},{6,7},{8,9},{9,10},{10,11},{11... | collective-permute-start | bytes 393224 | tf_op jit(solution)/shard_map/ppermute | solution.py:20
  30.4 3.7 %copy-start.7 = (f32[16,32,1024]{2,1,0:T(8,128)S(1)}, f32[16,32,1024]{2,1,0:T(8,128)}, u32[]{:S(2)}) copy-start(f32[16,32,1024]{2,1,0:T(8,128)} %copy-done.6) | copy-start | bytes 6291460
  30.4 3.7 %copy-start.9 = (bf16[1,16,32,1024]{3,2,1,0:T(8,128)(2,1)S(1)}, bf16[1,16,32,1024]{3,2,1,0:T(8,128)(2,1)}, u32[]{:S(2)}) copy-start(bf16[1,16,32,1024]{3,2,1,0:T(8,128)(2,1)} %param.8) | copy-start | bytes 3145732
  34.1 13.1 %copy-start.17 = (f32[1,256,128]{1,2,0:T(8,128)S(1)}, f32[1,256,128]{1,2,0:T(8,128)}, u32[]{:S(2)}) copy-start(f32[1,256,128]{1,2,0:T(8,128)} %copy.21) | copy-start | bytes 393220
  38.8 1.3 copy-start.4
  40.9 10.9 %collective-permute-start.4 = (f32[1,32,1024]{2,1,0:T(8,128)}, f32[1,32,1024]{2,1,0:T(8,128)}, u32[]{:S(2)}, u32[]{:S(2)}) collective-permute-start(f32[1,32,1024]{2,1,0:T(8,128)} %get-tuple-element.18), channel_id=1, source_target_pairs={{1,0},{2,1},{3,2},{4,3},{5,4},{6,5},{7,6},{9,8},{10,9},{11,10},{12... | collective-permute-start | bytes 393224 | tf_op jit(solution)/shard_map/ppermute | solution.py:22
  42.8 9.0 %collective-permute-start.5 = (f32[1,32,1024]{2,1,0:T(8,128)}, f32[1,32,1024]{2,1,0:T(8,128)}, u32[]{:S(2)}, u32[]{:S(2)}) collective-permute-start(f32[1,32,1024]{2,1,0:T(8,128)} %get-tuple-element.17), channel_id=1, source_target_pairs={{0,1},{1,2},{2,3},{3,4},{4,5},{5,6},{6,7},{8,9},{9,10},{10,11},{11... | collective-permute-start | bytes 393224 | tf_op jit(solution)/shard_map/ppermute | solution.py:20
  48.1 19.2 %all-to-all-start = ((f32[8,16,128]{2,1,0:T(8,128)}), f32[8,16,128]{2,1,0:T(8,128)S(1)}, u32[]{:S(2)}, u32[]{:S(2)}) async-start(f32[8,16,128]{2,1,0:T(8,128)} %fusion.37), calls=%async_computation | async-start | bytes 131072 | tf_op jit(solution)/shard_map/all_to_all | solution.py:44
  51.8 2.4 %copy-start.5 = (f32[16,32,1024]{2,1,0:T(8,128)S(1)}, f32[16,32,1024]{2,1,0:T(8,128)}, u32[]{:S(2)}) copy-start(f32[16,32,1024]{2,1,0:T(8,128)} %copy-done.4) | copy-start | bytes 6291460
  51.8 2.6 %copy-start.10 = (bf16[1,16,32,1024]{3,2,1,0:T(8,128)(2,1)S(1)}, bf16[1,16,32,1024]{3,2,1,0:T(8,128)(2,1)}, u32[]{:S(2)}) copy-start(bf16[1,16,32,1024]{3,2,1,0:T(8,128)(2,1)} %param.8) | copy-start | bytes 3145732
  54.4 12.3 %copy-start.18 = (s32[1,256]{1,0:T(1,128)S(1)}, s32[1,256]{1,0:T(1,128)}, u32[]{:S(2)}) copy-start(s32[1,256]{1,0:T(1,128)} %param.11) | copy-start | bytes 3076
  59.1 1.3 copy-start.2
  61.1 18.2 %collective-permute-start.6 = (f32[1,32,1024]{2,1,0:T(8,128)}, f32[1,32,1024]{2,1,0:T(8,128)}, u32[]{:S(2)}, u32[]{:S(2)}) collective-permute-start(f32[1,32,1024]{2,1,0:T(8,128)} %get-tuple-element.16), channel_id=1, source_target_pairs={{1,0},{2,1},{3,2},{4,3},{5,4},{6,5},{7,6},{9,8},{10,9},{11,10},{12... | collective-permute-start | bytes 393224 | tf_op jit(solution)/shard_map/ppermute | solution.py:22
  63.0 16.3 %collective-permute-start.7 = (f32[1,32,1024]{2,1,0:T(8,128)}, f32[1,32,1024]{2,1,0:T(8,128)}, u32[]{:S(2)}, u32[]{:S(2)}) collective-permute-start(f32[1,32,1024]{2,1,0:T(8,128)} %get-tuple-element.15), channel_id=1, source_target_pairs={{0,1},{1,2},{2,3},{3,4},{4,5},{5,6},{6,7},{8,9},{9,10},{10,11},{11... | collective-permute-start | bytes 393224 | tf_op jit(solution)/shard_map/ppermute | solution.py:20
  68.0 40.4 %all-to-all-start.1 = ((f32[32,16,128]{2,1,0:T(8,128)}), f32[32,16,128]{2,1,0:T(8,128)}, u32[]{:S(2)}, u32[]{:S(2)}) async-start(f32[32,16,128]{2,1,0:T(8,128)} %broadcast_in_dim.51), calls=%async_computation.1 | async-start | bytes 524288 | tf_op jit(solution)/shard_map/all_to_all | solution.py:38
  79.3 2.4 %copy-start.3 = (f32[16,32,1024]{2,1,0:T(8,128)S(1)}, f32[16,32,1024]{2,1,0:T(8,128)}, u32[]{:S(2)}) copy-start(f32[16,32,1024]{2,1,0:T(8,128)} %copy-done.2) | copy-start | bytes 6291460
  79.4 2.6 %copy-start.11 = (bf16[1,16,32,1024]{3,2,1,0:T(8,128)(2,1)S(1)}, bf16[1,16,32,1024]{3,2,1,0:T(8,128)(2,1)}, u32[]{:S(2)}) copy-start(bf16[1,16,32,1024]{3,2,1,0:T(8,128)(2,1)} %param.8) | copy-start | bytes 3145732
  81.9 11.8 %copy-start.22 = (s32[256,1]{0,1:T(1,128)S(1)}, s32[256,1]{0,1:T(1,128)}, u32[]{:S(2)}) copy-start(s32[256,1]{0,1:T(1,128)} %compare_select_fusion.1) | copy-start | bytes 3076
  81.9 31.5 %copy-start.19 = (s32[1,256]{1,0:T(1,128)S(1)}, s32[1,256]{1,0:T(1,128)}, u32[]{:S(2)}) copy-start(s32[1,256]{1,0:T(1,128)} %param.11) | copy-start | bytes 3076
  81.9 31.5 %copy-start.21 = (f32[1,256]{1,0:T(1,128)S(1)}, f32[1,256]{1,0:T(1,128)}, u32[]{:S(2)}) copy-start(f32[1,256]{1,0:T(1,128)} %param.10) | copy-start | bytes 3076
  86.7 1.3 copy-start.12
  88.5 6.5 %collective-permute-start.8 = (f32[1,256]{1,0:T(1,128)S(1)}, f32[1,256]{1,0:T(1,128)S(1)}, u32[]{:S(2)}, u32[]{:S(2)}) collective-permute-start(f32[1,256]{1,0:T(1,128)S(1)} %div.18), channel_id=1, source_target_pairs={{0,128},{8,136},{16,144},{24,152},{32,160},{40,168},{48,176},{56,1... | collective-permute-start | bytes 3080 | tf_op jit(solution)/shard_map/ppermute | solution.py:32
  110.0 8.3 %all-to-all-start.2 = ((f32[8,16,128]{2,1,0:T(8,128)}), f32[8,16,128]{2,1,0:T(8,128)S(1)}, u32[]{:S(2)}, u32[]{:S(2)}) async-start(f32[8,16,128]{2,1,0:T(8,128)} %broadcast_in_dim.52), calls=%async_computation.2 | async-start | bytes 131072 | tf_op jit(solution)/shard_map/all_to_all | solution.py:47
  119.0 35.4 %all-to-all-start.3 = ((f32[256,1,128]{2,1,0:T(1,128)}), f32[256,1,128]{2,1,0:T(1,128)S(1)}, u32[]{:S(2)}, u32[]{:S(2)}) async-start(f32[256,1,128]{2,1,0:T(1,128)} %broadcast_in_dim.54), calls=%async_computation.3 | async-start | bytes 262144 | tf_op jit(solution)/shard_map/all_to_all | solution.py:38
where the time goes:
time: 156 us
  starting transfers between devices  59.9 us (38%)
  other arithmetic  56.9 us (36%)
  local copies, waits for them, and re-layouts  16.7 us (11%)
  blocking collectives  11.7 us (8%)
  waiting for transfers between devices  7.42 us (5%)
  matrix products  1.95 us (1%)
    all_to_all x2, starting transfers between devices, gather_sum(): return jnp.sum(lax.all_to_all(copies, axes, 0, 0, tiled=True), axis=0)  22.6 us
    add x4, other arithmetic, march_forward(): centre + STEP_SIZE * (diffuse_subdomain.astype(jnp.float32) * spread - ca...  21.2 us
    ppermute x4, starting transfers between devices, padded(): lax.ppermute(tail, axis, [(i, (i + 1) % count) for i in range(ends)])  13.4 us
    another operation x3, other arithmetic, shards(): lower_factor = jnp.linalg.cholesky(gram_matrix)  12.4 us
    all_gather x1, blocking collectives, shards(): partner_all = lax.all_gather(partner_own, 'slab', axis=1, tiled=True)  11.7 us
    ppermute x4, starting transfers between devices, padded(): lax.ppermute(head, axis, [((i + 1) % count, i) for i in range(ends)])  11.4 us
    another operation x2, other arithmetic, shards(): lax.linalg.triangular_solve(lower_factor, half_solve, left_side=True, low...  10.5 us
    concatenate x4, other arithmetic, surround_wrapper(): jnp.concatenate([bottom, block_rows, mirror_layer[:, None, :]], axis=1)  9.12 us
  transfers between devices with their start and end apart: 13, of which 4 were waited for; matrix products, arithmetic and copies ran while one was open for 30% of the time, Pallas kernels for 0%

commit v1 on v0

--- a/solution.py
+++ b/solution.py
@@ -117,7 +117,18 @@
     face_means = face_means.reshape(1, rows_dev)
     top_bit = lax.axis_size("wide").bit_length() - 2
     partner_own = partner(face_means, "wide", top_bit)
-    partner_all = lax.all_gather(partner_own, "slab", axis=1, tiled=True)
+    ways = lax.axis_size("slab")
+    up = [(d, (d + 1) % ways) for d in range(ways)]
+    down = [(d, (d - 1) % ways) for d in range(ways)]
+    earlier, later = ([partner_own], [partner_own])
+    for _ in range(ways // 2):
+        earlier.append(lax.ppermute(earlier[-1], "slab", up))
+    for _ in range((ways - 1) // 2):
+        later.append(lax.ppermute(later[-1], "slab", down))
+    line = jnp.concatenate([*earlier[::-1], *later[1:]], axis=1)
+    partner_all = jnp.roll(
+        line, (lax.axis_index("slab") - ways // 2) * partner_own.shape[1], axis=1
+    )
     tilde = jnp.take(partner_all[0], partner_facing_rows[0], axis=0)
     resid = tilde - interface_guess[0]
     proj_local = jnp.dot(

time: 156 us -> 152 us (0.974)
  waiting for transfers between devices: 7.42 us -> 19.7 us
  blocking collectives: 11.7 us -> 0 us
  starting transfers between devices: 59.9 us -> 69.8 us
  local copies, waits for them, and re-layouts: 16.7 us -> 7.8 us
  other arithmetic: 56.9 us -> 50.9 us
    all_gather x1 -> x0, blocking collectives: 11.7 us -> none  [shards(): partner_all = lax.all_gather(partner_own, 'slab', axis=1, tiled=True)]
    ppermute x0 -> x7, starting transfers between devices: none -> 11 us  [the longest x4 9.48 us: shards(): earlier.append(lax.ppermute(earlier[-1], 'slab', up))]
    unnamed x49 -> x34, local copies, waits for them, and re-layouts: 8.98 us -> 2.01 us
    all_to_all x2, starting transfers between devices: 22.6 us -> 15.7 us  [gather_sum(): return jnp.sum(lax.all_to_all(copies, axes, 0, 0, tiled=True), axis=0)]
    all_to_all x2, waiting for transfers between devices: 0.01 us -> 5.74 us  [gather_sum(): return jnp.sum(lax.all_to_all(copies, axes, 0, 0, tiled=True), axis=0)]
    concatenate x4, other arithmetic: 9.12 us -> 4.21 us  [surround_wrapper(): jnp.concatenate([bottom, block_rows, mirror_layer[:, None, :]], axis=1)]
    all_to_all x1, starting transfers between devices: 3.44 us -> 6.7 us  [sum_everywhere(): lax.all_to_all(copies, 'slab', 0, 0, tiled=True).reshape(square.shape)]
    ppermute x0 -> x7, waiting for transfers between devices: none -> 2.83 us  [the longest x3 1.69 us: shards(): later.append(lax.ppermute(later[-1], 'slab', down))]
  transfers between devices with their start and end apart: 13 -> 20, of which waited for: 4 -> 13; matrix products, arithmetic and copies ran while one was open for 30% -> 20% of each run, Pallas kernels for 0% -> 0%
where the time goes in v1:
time: 152 us; the launch traced here: 151 us
  starting transfers between devices  69.8 us (46%)
  other arithmetic  50.9 us (33%)
  waiting for transfers between devices  19.7 us (13%)
  local copies, waits for them, and re-layouts  7.8 us (5%)
  matrix products  1.96 us (1%)
    add x4, other arithmetic, march_forward(): centre + STEP_SIZE * (diffuse_subdomain.astype(jnp.float32) * spread - ca...  21.7 us
    all_to_all x2, starting transfers between devices, gather_sum(): return jnp.sum(lax.all_to_all(copies, axes, 0, 0, tiled=True), axis=0)  15.7 us
    ppermute x4, starting transfers between devices, padded(): lax.ppermute(tail, axis, [(i, (i + 1) % count) for i in range(ends)])  14.3 us
    another operation x3, other arithmetic, shards(): lower_factor = jnp.linalg.cholesky(gram_matrix)  12.4 us
    ppermute x4, starting transfers between devices, padded(): lax.ppermute(head, axis, [((i + 1) % count, i) for i in range(ends)])  11.4 us
    another operation x2, other arithmetic, shards(): lax.linalg.triangular_solve(lower_factor, half_solve, left_side=True, low...  10.5 us
    ppermute x4, starting transfers between devices, shards(): earlier.append(lax.ppermute(earlier[-1], 'slab', up))  9.48 us
    all_to_all x1, starting transfers between devices, sum_everywhere(): lax.all_to_all(copies, 'slab', 0, 0, tiled=True).reshape(square.shape)  6.7 us
  transfers between devices with their start and end apart: 20, of which 13 were waited for; matrix products, arithmetic and copies ran while one was open for 20% of the time, Pallas kernels for 0%

profile of v1, /device:TPU:1, one launch (start us, length us, event | category | flops | bytes accessed | tf_op | source)
XLA Modules:
  0.0 151.3 jit_solution(6239049017597496087)
XLA Ops:
  0.7 1.1 slice_bitcast_fusion
  1.8 5.1 %collective-permute-start = (f32[1,32,1024]{2,1,0:T(8,128)S(1)}, f32[1,32,1024]{2,1,0:T(8,128)S(1)}, u32[]{:S(2)}, u32[]{:S(2)}) collective-permute-start(f32[1,32,1024]{2,1,0:T(8,128)S(1)} %get-tuple-element.22), channel_id=1, source_target_pairs={{1,0},{2,1},{3,2},{4,3},{5,4},{6,5},{7,6},{9,8},{10,9},{11,10},{12... | collective-permute-start | bytes 393224 | tf_op jit(solution)/shard_map/ppermute | solution.py:22
  7.0 1.9 %collective-permute-start.1 = (f32[1,32,1024]{2,1,0:T(8,128)S(1)}, f32[1,32,1024]{2,1,0:T(8,128)S(1)}, u32[]{:S(2)}, u32[]{:S(2)}) collective-permute-start(f32[1,32,1024]{2,1,0:T(8,128)S(1)} %get-tuple-element.21), channel_id=1, source_target_pairs={{0,1},{1,2},{2,3},{3,4},{4,5},{5,6},{6,7},{8,9},{9,10},{10,11},{11... | collective-permute-start | bytes 393224 | tf_op jit(solution)/shard_map/ppermute | solution.py:20
  9.4 1.3 reduce.12
  11.2 2.3 %pad_maximum_fusion.3 = f32[18,34,1024]{2,1,0:T(8,128)S(1)} fusion(f32[18,1,1024]{2,1,0:T(1,128)S(1)} %broadcast_in_dim.48, f32[1,32,1024]{2,1,0:T(8,128)S(1)} %collective-permute-done, f32[16,32,1024]{2,1,0:T(8,128)} %bitcast.102, f32[1,32,1024]{2,1,0:T(8,128)S(1)} %collective-permute-done.1, f32[34]{0:T(128)S(1)} %pad.74.clone), kind=kLoop, calls=%fused_computation.4 | loop fusion | flops 2506752 | bytes 4939912 | tf_op jit(solution)/shard_map/concatenate | solution.py:52
  13.9 5.4 %fusion.2 = f32[16,32,1024]{2,1,0:T(8,128)S(1)} fusion(f32[16,32,1024]{2,1,0:T(8,128)S(1)} %bitcast.103, f32[18,34,1024]{2,1,0:T(8,128)S(1)} %pad_maximum_fusion.3, f32[1,32,1024]{2,1,0:T(8,128)S(1)} %collective-permute-done, f32[1,32,1024]{2,1,0:T(8,128)S(1)} %collective-permute-done.1, f32[18,1,1024]{2,1,0:T(1,128)S(1)} %broadcast_in_dim.48, ...), kind=kLoop, calls=%fused_computation.35 | loop fusion | flops 18874368 | bytes 11231232 | tf_op jit(solution)/shard_map/add | solution.py:78
  19.4 2.4 %collective-permute-start.2 = (f32[1,32,1024]{2,1,0:T(8,128)S(1)}, f32[1,32,1024]{2,1,0:T(8,128)S(1)}, u32[]{:S(2)}, u32[]{:S(2)}) collective-permute-start(f32[1,32,1024]{2,1,0:T(8,128)S(1)} %get-tuple-element.20), channel_id=1, source_target_pairs={{1,0},{2,1},{3,2},{4,3},{5,4},{6,5},{7,6},{9,8},{10,9},{11,10},{12... | collective-permute-start | bytes 393224 | tf_op jit(solution)/shard_map/ppermute | solution.py:22
  21.8 3.5 %collective-permute-start.3 = (f32[1,32,1024]{2,1,0:T(8,128)S(1)}, f32[1,32,1024]{2,1,0:T(8,128)S(1)}, u32[]{:S(2)}, u32[]{:S(2)}) collective-permute-start(f32[1,32,1024]{2,1,0:T(8,128)S(1)} %get-tuple-element.19), channel_id=1, source_target_pairs={{0,1},{1,2},{2,3},{3,4},{4,5},{5,6},{6,7},{8,9},{9,10},{10,11},{11... | collective-permute-start | bytes 393224 | tf_op jit(solution)/shard_map/ppermute | solution.py:20
  25.4 0.7 collective-permute-done.2
  26.1 1.2 collective-permute-done.3
  27.3 0.6 pad_maximum_fusion.2
  27.9 5.4 %fusion.5 = f32[16,32,1024]{2,1,0:T(8,128)S(1)} fusion(f32[16,32,1024]{2,1,0:T(8,128)S(1)} %fusion.2, f32[18,34,1024]{2,1,0:T(8,128)S(1)} %pad_maximum_fusion.2, f32[1,32,1024]{2,1,0:T(8,128)S(1)} %collective-permute-done.2, f32[1,32,1024]{2,1,0:T(8,128)S(1)} %collective-permute-done.3, f32[18,1,1024]{2,1,0:T(1,128)S(1)} %broadcast_in_dim.48, ...), kind=kLoop, calls=%fused_computation.38 | loop fusion | flops 18874368 | bytes 11231232 | tf_op jit(solution)/shard_map/add | solution.py:78
  33.4 1.9 %collective-permute-start.4 = (f32[1,32,1024]{2,1,0:T(8,128)S(1)}, f32[1,32,1024]{2,1,0:T(8,128)S(1)}, u32[]{:S(2)}, u32[]{:S(2)}) collective-permute-start(f32[1,32,1024]{2,1,0:T(8,128)S(1)} %get-tuple-element.18), channel_id=1, source_target_pairs={{1,0},{2,1},{3,2},{4,3},{5,4},{6,5},{7,6},{9,8},{10,9},{11,10},{12... | collective-permute-start | bytes 393224 | tf_op jit(solution)/shard_map/ppermute | solution.py:22
  35.3 4.4 %collective-permute-start.5 = (f32[1,32,1024]{2,1,0:T(8,128)S(1)}, f32[1,32,1024]{2,1,0:T(8,128)S(1)}, u32[]{:S(2)}, u32[]{:S(2)}) collective-permute-start(f32[1,32,1024]{2,1,0:T(8,128)S(1)} %get-tuple-element.17), channel_id=1, source_target_pairs={{0,1},{1,2},{2,3},{3,4},{4,5},{5,6},{6,7},{8,9},{9,10},{10,11},{11... | collective-permute-start | bytes 393224 | tf_op jit(solution)/shard_map/ppermute | solution.py:20
  39.7 0.7 collective-permute-done.4
  40.4 1.2 collective-permute-done.5
  41.6 0.6 pad_maximum_fusion.1
  42.3 5.4 %fusion.8 = f32[16,32,1024]{2,1,0:T(8,128)S(1)} fusion(f32[16,32,1024]{2,1,0:T(8,128)S(1)} %fusion.5, f32[18,34,1024]{2,1,0:T(8,128)S(1)} %pad_maximum_fusion.1, f32[1,32,1024]{2,1,0:T(8,128)S(1)} %collective-permute-done.4, f32[1,32,1024]{2,1,0:T(8,128)S(1)} %collective-permute-done.5, f32[18,1,1024]{2,1,0:T(1,128)S(1)} %broadcast_in_dim.48, ...), kind=kLoop, calls=%fused_computation.41 | loop fusion | flops 18874368 | bytes 11231232 | tf_op jit(solution)/shard_map/add | solution.py:78
  47.7 1.9 %collective-permute-start.6 = (f32[1,32,1024]{2,1,0:T(8,128)S(1)}, f32[1,32,1024]{2,1,0:T(8,128)S(1)}, u32[]{:S(2)}, u32[]{:S(2)}) collective-permute-start(f32[1,32,1024]{2,1,0:T(8,128)S(1)} %get-tuple-element.16), channel_id=1, source_target_pairs={{1,0},{2,1},{3,2},{4,3},{5,4},{6,5},{7,6},{9,8},{10,9},{11,10},{12... | collective-permute-start | bytes 393224 | tf_op jit(solution)/shard_map/ppermute | solution.py:22
  49.6 4.5 %collective-permute-start.7 = (f32[1,32,1024]{2,1,0:T(8,128)S(1)}, f32[1,32,1024]{2,1,0:T(8,128)S(1)}, u32[]{:S(2)}, u32[]{:S(2)}) collective-permute-start(f32[1,32,1024]{2,1,0:T(8,128)S(1)} %get-tuple-element.15), channel_id=1, source_target_pairs={{0,1},{1,2},{2,3},{3,4},{4,5},{5,6},{6,7},{8,9},{9,10},{10,11},{11... | collective-permute-start | bytes 393224 | tf_op jit(solution)/shard_map/ppermute | solution.py:20
  54.7 1.2 collective-permute-done.7
  55.9 0.7 pad_maximum_fusion
  56.6 5.4 %fusion.11 = f32[16,32,1024]{2,1,0:T(8,128)S(1)} fusion(f32[16,32,1024]{2,1,0:T(8,128)S(1)} %fusion.8, f32[18,34,1024]{2,1,0:T(8,128)S(1)} %pad_maximum_fusion, f32[1,32,1024]{2,1,0:T(8,128)S(1)} %collective-permute-done.6, f32[1,32,1024]{2,1,0:T(8,128)S(1)} %collective-permute-done.7, f32[18,1,1024]{2,1,0:T(1,128)S(1)} %broadcast_in_dim.48, ...), kind=kLoop, calls=%fused_computation.44 | loop fusion | flops 18874368 | bytes 11231232 | tf_op jit(solution)/shard_map/add | solution.py:78
  62.5 6.3 %collective-permute-start.8 = (f32[1,256]{1,0:T(1,128)S(1)}, f32[1,256]{1,0:T(1,128)S(1)}, u32[]{:S(2)}, u32[]{:S(2)}) collective-permute-start(f32[1,256]{1,0:T(1,128)S(1)} %div.18), channel_id=1, source_target_pairs={{0,128},{8,136},{16,144},{24,152},{32,160},{40,168},{48,176},{56,1... | collective-permute-start | bytes 3080 | tf_op jit(solution)/shard_map/ppermute | solution.py:32
  68.9 0.9 collective-permute-done.8
  69.8 3.3 %collective-permute-start.9 = (f32[1,256]{1,0:T(1,128)S(1)}, f32[1,256]{1,0:T(1,128)S(1)}, u32[]{:S(2)}, u32[]{:S(2)}) collective-permute-start(f32[1,256]{1,0:T(1,128)S(1)} %collective-permute-done.8), channel_id=1, source_target_pairs={{0,1},{1,2},{2,3},{3,4},{4,5},{5,6},{6,7},{7,0},{8,9},{9,10},{10,1... | collective-permute-start | bytes 3080 | tf_op jit(solution)/shard_map/ppermute | solution.py:125
  73.1 0.9 fusion.37
  74.0 4.4 %all-to-all-start = ((f32[8,16,128]{2,1,0:T(8,128)}), f32[8,16,128]{2,1,0:T(8,128)S(1)}, u32[]{:S(2)}, u32[]{:S(2)}) async-start(f32[8,16,128]{2,1,0:T(8,128)} %fusion.37), calls=%async_computation | async-start | bytes 131072 | tf_op jit(solution)/shard_map/all_to_all | solution.py:44
  78.4 1.6 %collective-permute-start.10 = (f32[1,256]{1,0:T(1,128)S(1)}, f32[1,256]{1,0:T(1,128)S(1)}, u32[]{:S(2)}, u32[]{:S(2)}) collective-permute-start(f32[1,256]{1,0:T(1,128)S(1)} %collective-permute-done.9), channel_id=1, source_target_pairs={{0,1},{1,2},{2,3},{3,4},{4,5},{5,6},{6,7},{7,0},{8,9},{9,10},{10,1... | collective-permute-start | bytes 3080 | tf_op jit(solution)/shard_map/ppermute | solution.py:125
  80.0 0.7 collective-permute-done.10
  80.7 2.3 %collective-permute-start.11 = (f32[1,256]{1,0:T(1,128)S(1)}, f32[1,256]{1,0:T(1,128)S(1)}, u32[]{:S(2)}, u32[]{:S(2)}) collective-permute-start(f32[1,256]{1,0:T(1,128)S(1)} %collective-permute-done.10), channel_id=1, source_target_pairs={{0,1},{1,2},{2,3},{3,4},{4,5},{5,6},{6,7},{7,0},{8,9},{9,10},{10,1... | collective-permute-start | bytes 3080 | tf_op jit(solution)/shard_map/ppermute | solution.py:125
  83.7 2.3 %collective-permute-start.12 = (f32[1,256]{1,0:T(1,128)S(1)}, f32[1,256]{1,0:T(1,128)S(1)}, u32[]{:S(2)}, u32[]{:S(2)}) collective-permute-start(f32[1,256]{1,0:T(1,128)S(1)} %collective-permute-done.11), channel_id=1, source_target_pairs={{0,1},{1,2},{2,3},{3,4},{4,5},{5,6},{6,7},{7,0},{8,9},{9,10},{10,1... | collective-permute-start | bytes 3080 | tf_op jit(solution)/shard_map/ppermute | solution.py:125
  86.0 0.7 broadcast_in_dim.51
  86.7 9.9 %all-to-all-start.1 = ((f32[32,16,128]{2,1,0:T(8,128)}), f32[32,16,128]{2,1,0:T(8,128)S(1)}, u32[]{:S(2)}, u32[]{:S(2)}) async-start(f32[32,16,128]{2,1,0:T(8,128)} %broadcast_in_dim.51), calls=%async_computation.1 | async-start | bytes 524288 | tf_op jit(solution)/shard_map/all_to_all | solution.py:38
  96.7 1.5 %collective-permute-start.15 = (f32[1,256]{1,0:T(1,128)S(1)}, f32[1,256]{1,0:T(1,128)S(1)}, u32[]{:S(2)}, u32[]{:S(2)}) collective-permute-start(f32[1,256]{1,0:T(1,128)S(1)} %collective-permute-done.14), channel_id=1, source_target_pairs={{0,7},{1,0},{2,1},{3,2},{4,3},{5,4},{6,5},{7,6},{8,15},{9,8},{10,9... | collective-permute-start | bytes 3080 | tf_op jit(solution)/shard_map/ppermute | solution.py:127
  98.3 1.4 collective-permute-done.15
  99.8 1.7 %gather_fusion = f32[256]{0:T(256)S(1)} fusion(f32[2048]{0:T(1024)S(1)} %bitcast.101, s32[1024]{0:T(1024)S(1)} %pad_clamp_fusion), kind=kCustom, calls=%fused_computation | custom fusion | bytes 3072 | tf_op jit(solution)/shard_map/jit(_take)/gather | solution.py:132
  101.5 5.7 %all-to-all-done.1 = f32[32,16,128]{2,1,0:T(8,128)S(1)} async-done(((f32[32,16,128]{2,1,0:T(8,128)}), f32[32,16,128]{2,1,0:T(8,128)S(1)}, u32[]{:S(2)}, u32[]{:S(2)}) %all-to-all-start.1) | async-done | bytes 262176 | tf_op jit(solution)/shard_map/all_to_all | solution.py:38
  107.3 0.6 broadcast_in_dim.52
  108.0 6.7 %all-to-all-start.2 = ((f32[8,16,128]{2,1,0:T(8,128)}), f32[8,16,128]{2,1,0:T(8,128)S(1)}, u32[]{:S(2)}, u32[]{:S(2)}) async-start(f32[8,16,128]{2,1,0:T(8,128)} %broadcast_in_dim.52), calls=%async_computation.2 | async-start | bytes 131072 | tf_op jit(solution)/shard_map/all_to_all | solution.py:47
  114.8 4.7 %all-to-all-done.2 = f32[8,16,128]{2,1,0:T(8,128)S(1)} async-done(((f32[8,16,128]{2,1,0:T(8,128)}), f32[8,16,128]{2,1,0:T(8,128)S(1)}, u32[]{:S(2)}, u32[]{:S(2)}) %all-to-all-start.2) | async-done | bytes 65568 | tf_op jit(solution)/shard_map/all_to_all | solution.py:47
  119.5 0.7 broadcast_in_dim.54
  120.2 5.8 %all-to-all-start.3 = ((f32[256,1,128]{2,1,0:T(1,128)}), f32[256,1,128]{2,1,0:T(1,128)S(1)}, u32[]{:S(2)}, u32[]{:S(2)}) async-start(f32[256,1,128]{2,1,0:T(1,128)} %broadcast_in_dim.54), calls=%async_computation.3 | async-start | bytes 262144 | tf_op jit(solution)/shard_map/all_to_all | solution.py:38
  126.1 11.7 %cholesky.16 = f32[128,128]{1,0:T(8,128)S(1)} custom-call(f32[128,128]{1,0:T(8,128)S(1)} %fusion.45), custom_call_target="Cholesky" | custom-call | tf_op jit(solution)/shard_map/jit(cholesky)/cholesky | solution.py:139
  137.9 0.6 compare_reduce_fusion
  138.5 0.7 fusion.41
  139.2 9.8 %custom-call.10 = f32[1,128,128]{1,2,0:T(8,128)S(1)} custom-call(f32[1,128,128]{2,1,0:T(8,128)S(1)} %fusion.41), custom_call_target="InvertDiagBlocksLowerTriangular" | custom-call | tf_op jit(solution)/shard_map/triangular_solve | solution.py:143
  149.3 0.8 copy.25
  (75 shorter events, 5.3 us)
Async XLA Ops:
  0.6 149.8 %copy-start = (f32[1,256,128]{2,1,0:T(8,128)S(1)}, f32[1,256,128]{2,1,0:T(8,128)}, u32[]{:S(2)}) copy-start(f32[1,256,128]{2,1,0:T(8,128)} %param.13) | copy-start | bytes 393220
  0.6 12.8 %copy-start.3 = (f32[1,16,32,1024]{3,2,1,0:T(8,128)S(1)}, f32[1,16,32,1024]{3,2,1,0:T(8,128)}, u32[]{:S(2)}) copy-start(f32[1,16,32,1024]{3,2,1,0:T(8,128)} %param.7) | copy-start | bytes 6291460
  1.8 9.3 %collective-permute-start = (f32[1,32,1024]{2,1,0:T(8,128)S(1)}, f32[1,32,1024]{2,1,0:T(8,128)S(1)}, u32[]{:S(2)}, u32[]{:S(2)}) collective-permute-start(f32[1,32,1024]{2,1,0:T(8,128)S(1)} %get-tuple-element.22), channel_id=1, source_target_pairs={{1,0},{2,1},{3,2},{4,3},{5,4},{6,5},{7,6},{9,8},{10,9},{11,10},{12... | collective-permute-start | bytes 393224 | tf_op jit(solution)/shard_map/ppermute | solution.py:22
  7.0 4.2 %collective-permute-start.1 = (f32[1,32,1024]{2,1,0:T(8,128)S(1)}, f32[1,32,1024]{2,1,0:T(8,128)S(1)}, u32[]{:S(2)}, u32[]{:S(2)}) collective-permute-start(f32[1,32,1024]{2,1,0:T(8,128)S(1)} %get-tuple-element.21), channel_id=1, source_target_pairs={{0,1},{1,2},{2,3},{3,4},{4,5},{5,6},{6,7},{8,9},{9,10},{10,11},{11... | collective-permute-start | bytes 393224 | tf_op jit(solution)/shard_map/ppermute | solution.py:20
  11.1 2.5 %copy-start.1 = (bf16[3,1,16,32,1024]{4,3,2,1,0:T(8,128)(2,1)S(1)}, bf16[3,1,16,32,1024]{4,3,2,1,0:T(8,128)(2,1)}, u32[]{:S(2)}) copy-start(bf16[3,1,16,32,1024]{4,3,2,1,0:T(8,128)(2,1)} %param.9) | copy-start | bytes 9437188
  11.1 2.8 %copy-start.2 = (bf16[1,16,32,1024]{3,2,1,0:T(8,128)(2,1)S(1)}, bf16[1,16,32,1024]{3,2,1,0:T(8,128)(2,1)}, u32[]{:S(2)}) copy-start(bf16[1,16,32,1024]{3,2,1,0:T(8,128)(2,1)} %param.8) | copy-start | bytes 3145732
  19.4 6.7 %collective-permute-start.2 = (f32[1,32,1024]{2,1,0:T(8,128)S(1)}, f32[1,32,1024]{2,1,0:T(8,128)S(1)}, u32[]{:S(2)}, u32[]{:S(2)}) collective-permute-start(f32[1,32,1024]{2,1,0:T(8,128)S(1)} %get-tuple-element.20), channel_id=1, source_target_pairs={{1,0},{2,1},{3,2},{4,3},{5,4},{6,5},{7,6},{9,8},{10,9},{11,10},{12... | collective-permute-start | bytes 393224 | tf_op jit(solution)/shard_map/ppermute | solution.py:22
  21.8 5.5 %collective-permute-start.3 = (f32[1,32,1024]{2,1,0:T(8,128)S(1)}, f32[1,32,1024]{2,1,0:T(8,128)S(1)}, u32[]{:S(2)}, u32[]{:S(2)}) collective-permute-start(f32[1,32,1024]{2,1,0:T(8,128)S(1)} %get-tuple-element.19), channel_id=1, source_target_pairs={{0,1},{1,2},{2,3},{3,4},{4,5},{5,6},{6,7},{8,9},{9,10},{10,11},{11... | collective-permute-start | bytes 393224 | tf_op jit(solution)/shard_map/ppermute | solution.py:20
  33.4 7.0 %collective-permute-start.4 = (f32[1,32,1024]{2,1,0:T(8,128)S(1)}, f32[1,32,1024]{2,1,0:T(8,128)S(1)}, u32[]{:S(2)}, u32[]{:S(2)}) collective-permute-start(f32[1,32,1024]{2,1,0:T(8,128)S(1)} %get-tuple-element.18), channel_id=1, source_target_pairs={{1,0},{2,1},{3,2},{4,3},{5,4},{6,5},{7,6},{9,8},{10,9},{11,10},{12... | collective-permute-start | bytes 393224 | tf_op jit(solution)/shard_map/ppermute | solution.py:22
  35.3 6.3 %collective-permute-start.5 = (f32[1,32,1024]{2,1,0:T(8,128)S(1)}, f32[1,32,1024]{2,1,0:T(8,128)S(1)}, u32[]{:S(2)}, u32[]{:S(2)}) collective-permute-start(f32[1,32,1024]{2,1,0:T(8,128)S(1)} %get-tuple-element.17), channel_id=1, source_target_pairs={{0,1},{1,2},{2,3},{3,4},{4,5},{5,6},{6,7},{8,9},{9,10},{10,11},{11... | collective-permute-start | bytes 393224 | tf_op jit(solution)/shard_map/ppermute | solution.py:20
  47.7 7.0 %collective-permute-start.6 = (f32[1,32,1024]{2,1,0:T(8,128)S(1)}, f32[1,32,1024]{2,1,0:T(8,128)S(1)}, u32[]{:S(2)}, u32[]{:S(2)}) collective-permute-start(f32[1,32,1024]{2,1,0:T(8,128)S(1)} %get-tuple-element.16), channel_id=1, source_target_pairs={{1,0},{2,1},{3,2},{4,3},{5,4},{6,5},{7,6},{9,8},{10,9},{11,10},{12... | collective-permute-start | bytes 393224 | tf_op jit(solution)/shard_map/ppermute | solution.py:22
  49.6 6.3 %collective-permute-start.7 = (f32[1,32,1024]{2,1,0:T(8,128)S(1)}, f32[1,32,1024]{2,1,0:T(8,128)S(1)}, u32[]{:S(2)}, u32[]{:S(2)}) collective-permute-start(f32[1,32,1024]{2,1,0:T(8,128)S(1)} %get-tuple-element.15), channel_id=1, source_target_pairs={{0,1},{1,2},{2,3},{3,4},{4,5},{5,6},{6,7},{8,9},{9,10},{10,11},{11... | collective-permute-start | bytes 393224 | tf_op jit(solution)/shard_map/ppermute | solution.py:20
  56.6 12.2 %copy-start.5 = (f32[1,256,128]{2,1,0:T(8,128)S(1)}, f32[1,256,128]{2,1,0:T(8,128)}, u32[]{:S(2)}) copy-start(f32[1,256,128]{2,1,0:T(8,128)} %param.12) | copy-start | bytes 393220
  56.6 23.4 %copy-start.6 = (s32[1,256]{1,0:T(1,128)S(1)}, s32[1,256]{1,0:T(1,128)}, u32[]{:S(2)}) copy-start(s32[1,256]{1,0:T(1,128)} %param.11) | copy-start | bytes 3076
  62.0 58.2 %copy-start.4 = (f32[16,32,1024]{2,1,0:T(8,128)}, f32[16,32,1024]{2,1,0:T(8,128)S(1)}, u32[]{:S(2)}) copy-start(f32[16,32,1024]{2,1,0:T(8,128)S(1)} %fusion.11) | copy-start | bytes 6291460
  62.0 52.6 %copy-start.7 = (f32[1,256]{1,0:T(1,128)S(1)}, f32[1,256]{1,0:T(1,128)}, u32[]{:S(2)}) copy-start(f32[1,256]{1,0:T(1,128)} %param.10) | copy-start | bytes 3076
  62.5 7.3 %collective-permute-start.8 = (f32[1,256]{1,0:T(1,128)S(1)}, f32[1,256]{1,0:T(1,128)S(1)}, u32[]{:S(2)}, u32[]{:S(2)}) collective-permute-start(f32[1,256]{1,0:T(1,128)S(1)} %div.18), channel_id=1, source_target_pairs={{0,128},{8,136},{16,144},{24,152},{32,160},{40,168},{48,176},{56,1... | collective-permute-start | bytes 3080 | tf_op jit(solution)/shard_map/ppermute | solution.py:32
  69.8 8.6 %collective-permute-start.9 = (f32[1,256]{1,0:T(1,128)S(1)}, f32[1,256]{1,0:T(1,128)S(1)}, u32[]{:S(2)}, u32[]{:S(2)}) collective-permute-start(f32[1,256]{1,0:T(1,128)S(1)} %collective-permute-done.8), channel_id=1, source_target_pairs={{0,1},{1,2},{2,3},{3,4},{4,5},{5,6},{6,7},{7,0},{8,9},{9,10},{10,1... | collective-permute-start | bytes 3080 | tf_op jit(solution)/shard_map/ppermute | solution.py:125
  74.0 12.0 %all-to-all-start = ((f32[8,16,128]{2,1,0:T(8,128)}), f32[8,16,128]{2,1,0:T(8,128)S(1)}, u32[]{:S(2)}, u32[]{:S(2)}) async-start(f32[8,16,128]{2,1,0:T(8,128)} %fusion.37), calls=%async_computation | async-start | bytes 131072 | tf_op jit(solution)/shard_map/all_to_all | solution.py:44
  78.4 2.4 %collective-permute-start.10 = (f32[1,256]{1,0:T(1,128)S(1)}, f32[1,256]{1,0:T(1,128)S(1)}, u32[]{:S(2)}, u32[]{:S(2)}) collective-permute-start(f32[1,256]{1,0:T(1,128)S(1)} %collective-permute-done.9), channel_id=1, source_target_pairs={{0,1},{1,2},{2,3},{3,4},{4,5},{5,6},{6,7},{7,0},{8,9},{9,10},{10,1... | collective-permute-start | bytes 3080 | tf_op jit(solution)/shard_map/ppermute | solution.py:125
  80.0 3.3 %collective-permute-start.13 = (f32[1,256]{1,0:T(1,128)S(1)}, f32[1,256]{1,0:T(1,128)S(1)}, u32[]{:S(2)}, u32[]{:S(2)}) collective-permute-start(f32[1,256]{1,0:T(1,128)S(1)} %collective-permute-done.8), channel_id=1, source_target_pairs={{0,7},{1,0},{2,1},{3,2},{4,3},{5,4},{6,5},{7,6},{8,15},{9,8},{10,9... | collective-permute-start | bytes 3080 | tf_op jit(solution)/shard_map/ppermute | solution.py:127
  80.7 3.0 %collective-permute-start.11 = (f32[1,256]{1,0:T(1,128)S(1)}, f32[1,256]{1,0:T(1,128)S(1)}, u32[]{:S(2)}, u32[]{:S(2)}) collective-permute-start(f32[1,256]{1,0:T(1,128)S(1)} %collective-permute-done.10), channel_id=1, source_target_pairs={{0,1},{1,2},{2,3},{3,4},{4,5},{5,6},{6,7},{7,0},{8,9},{9,10},{10,1... | collective-permute-start | bytes 3080 | tf_op jit(solution)/shard_map/ppermute | solution.py:125
  83.3 13.4 %collective-permute-start.14 = (f32[1,256]{1,0:T(1,128)S(1)}, f32[1,256]{1,0:T(1,128)S(1)}, u32[]{:S(2)}, u32[]{:S(2)}) collective-permute-start(f32[1,256]{1,0:T(1,128)S(1)} %collective-permute-done.13), channel_id=1, source_target_pairs={{0,7},{1,0},{2,1},{3,2},{4,3},{5,4},{6,5},{7,6},{8,15},{9,8},{10,9... | collective-permute-start | bytes 3080 | tf_op jit(solution)/shard_map/ppermute | solution.py:127
  83.7 14.5 %collective-permute-start.12 = (f32[1,256]{1,0:T(1,128)S(1)}, f32[1,256]{1,0:T(1,128)S(1)}, u32[]{:S(2)}, u32[]{:S(2)}) collective-permute-start(f32[1,256]{1,0:T(1,128)S(1)} %collective-permute-done.11), channel_id=1, source_target_pairs={{0,1},{1,2},{2,3},{3,4},{4,5},{5,6},{6,7},{7,0},{8,9},{9,10},{10,1... | collective-permute-start | bytes 3080 | tf_op jit(solution)/shard_map/ppermute | solution.py:125
  86.7 20.5 %all-to-all-start.1 = ((f32[32,16,128]{2,1,0:T(8,128)}), f32[32,16,128]{2,1,0:T(8,128)S(1)}, u32[]{:S(2)}, u32[]{:S(2)}) async-start(f32[32,16,128]{2,1,0:T(8,128)} %broadcast_in_dim.51), calls=%async_computation.1 | async-start | bytes 524288 | tf_op jit(solution)/shard_map/all_to_all | solution.py:38
  96.7 3.0 %collective-permute-start.15 = (f32[1,256]{1,0:T(1,128)S(1)}, f32[1,256]{1,0:T(1,128)S(1)}, u32[]{:S(2)}, u32[]{:S(2)}) collective-permute-start(f32[1,256]{1,0:T(1,128)S(1)} %collective-permute-done.14), channel_id=1, source_target_pairs={{0,7},{1,0},{2,1},{3,2},{4,3},{5,4},{6,5},{7,6},{8,15},{9,8},{10,9... | collective-permute-start | bytes 3080 | tf_op jit(solution)/shard_map/ppermute | solution.py:127
  108.0 11.5 %all-to-all-start.2 = ((f32[8,16,128]{2,1,0:T(8,128)}), f32[8,16,128]{2,1,0:T(8,128)S(1)}, u32[]{:S(2)}, u32[]{:S(2)}) async-start(f32[8,16,128]{2,1,0:T(8,128)} %broadcast_in_dim.52), calls=%async_computation.2 | async-start | bytes 131072 | tf_op jit(solution)/shard_map/all_to_all | solution.py:47
  120.2 29.8 %all-to-all-start.3 = ((f32[256,1,128]{2,1,0:T(1,128)}), f32[256,1,128]{2,1,0:T(1,128)S(1)}, u32[]{:S(2)}, u32[]{:S(2)}) async-start(f32[256,1,128]{2,1,0:T(1,128)} %broadcast_in_dim.54), calls=%async_computation.3 | async-start | bytes 262144 | tf_op jit(solution)/shard_map/all_to_all | solution.py:38
